TPU v7x, 32 devices: a whole 2x2x4 slice. The times are simulated.
32 devices in a mesh: task: 16 (over z, x, core), tensor: 2 (over y).
Axes of the slice: x: 2, y: 2, z: 4, core: 2. Of those that a mesh axis runs over, the one named last changes fastest.
Arguments:
- inputs: bfloat16 [3072, 8192], P('task'), may hold values from -6 to 6
- queries: bfloat16 [3072, 4096], P('task', 'tensor'), may hold values from -6 to 6
- task_vectors: bfloat16 [8, 2, 8192, 1024], P(None, None, 'task', 'tensor'), may hold values from -0.0625 to 0.0625
- base_weights: bfloat16 [2, 8192, 1024], P(None, 'task', 'tensor'), may hold values from -0.0625 to 0.0625
- scale_exps: int32 [8, 2, 64, 8], P(None, None, 'task', 'tensor'), may hold values from -3 to 0
- coefs: float32 [8, 2], replicated, may hold values from 0.1 to 0.6
Outputs:
- attended: bfloat16 [3072, 4096], P('task', 'tensor')
- mean_entropy: float32 [], replicated
- coef_grad: float32 [8, 2], replicated
All inputs are finite; a program needn't handle non-finite values.
Results may differ from a plain program's by a relative error of at most 0.0087.
Values may be sent and summed in bfloat16 or wider, within the bound.
A program may use at most 128 MiB of HBM per device.

v0:
```python
import functools
import math

import jax
import jax.numpy as jnp
from jax import lax
from jax.experimental import pallas as pl
from jax.experimental.pallas import tpu as pltpu
from jax.sharding import PartitionSpec as P

HEAD = 128
GROUP = 4

sharpen = 4.0
capping = 8.0
masked_value = -1e30

MESH = pl.DeviceIdType.MESH
VMEM_BYTES = 60 * 1024 * 1024
F32 = jnp.float32
BF16 = jnp.bfloat16


def factors(n_task):
    outer = math.gcd(n_task, 4)
    mid = math.gcd(n_task // outer, 2)
    return outer, mid, n_task // (outer * mid)


def place(dims):
    _, mid, inner = dims
    task = lax.axis_index("task")
    rest = lax.rem(task, mid * inner)
    return task, task // (mid * inner), rest // inner, lax.rem(rest, inner)


def turned(value, step, size):
    return lax.rem(value + (step + size), size)


def flip(value, step):
    bit = 1
    for_value = value
    while bit <= step:
        if step & bit:
            for_value = for_value + bit - 2 * bit * lax.rem(value // bit, 2)
        bit *= 2
    return for_value


def scale_of(exps, t, m, i, j):
    return lax.shift_left(jnp.int32(1), exps[m, i, j, t] + 3).astype(F32) * 0.125


def index_of(dims, a, b, c):
    _, mid, inner = dims
    return (a * mid + b) * inner + c


def meet(peers):
    sem = pltpu.get_barrier_semaphore()
    for peer in peers:
        pl.semaphore_signal(sem, inc=1, device_id=peer, device_id_type=MESH)
    pl.semaphore_wait(sem, len(peers))


def send(src, dst, send_sem, recv_sem, peer):
    copy = pltpu.make_async_remote_copy(
        src_ref=src,
        dst_ref=dst,
        send_sem=send_sem,
        recv_sem=recv_sem,
        device_id=peer,
        device_id_type=MESH,
    )
    copy.start()
    return copy


def fetch(src, dst, sem):
    copy = pltpu.make_async_copy(src, dst, sem)
    copy.start()
    return copy


def project_stage(
    dims, n_tensor, pieces,
    inputs, vectors, base, exps, coefs, greet,
    kv_out, rows_out,
    xin, mg, vec_v, base_v, acc, hold, pout, pin,
    local_sem, keep_sem, x_send, x_recv, y_send, y_recv, g_send, g_recv, r_send, r_recv, p_send, p_recv,
):
    outer, mid, inner = dims
    group = mid * inner
    task, a, b, c = place(dims)
    y = lax.axis_index("tensor")
    mine = b * inner + c
    tasks, mats, rows, cols = vectors.shape
    row_blocks, col_blocks = exps.shape[1:3]
    tokens = inputs.shape[0]
    piece = tokens // pieces
    span = group * rows
    part = span // n_tensor
    turns = list(range(outer - 1, 0, -1))

    def at(a_, b_, c_):
        return {"task": index_of(dims, a_, b_, c_), "tensor": y}

    def tensor_peer(step):
        return {"task": task, "tensor": turned(y, step, n_tensor)}

    def group_peer(f, e):
        return at(a, turned(b, f, mid), turned(c, e, inner))

    def some(k):
        return slice(k * piece, (k + 1) * piece)

    base_copy = fetch(base, base_v, local_sem.at[0])
    vec_copies = [
        fetch(vectors.at[:, m], vec_v.at[:, m], local_sem.at[2 + m]) for m in range(mats)
    ]
    own_copy = fetch(
        inputs.at[:, pl.ds(pl.multiple_of(a * span, 128), span)], xin.at[a], local_sem.at[1]
    )
    greet()
    sent = []
    x_copies = {}
    own_cols = pl.ds(pl.multiple_of(y * part, 128), part)
    for k in range(pieces):
        for d in turns:
            to = flip(a, d)
            slot = d * pieces + k
            x_copies[k, d] = send(
                inputs.at[some(k), pl.ds(pl.multiple_of(to * span + y * part, 128), part)],
                xin.at[a, some(k), own_cols],
                x_send.at[slot], x_recv.at[slot], at(to, b, c),
            )
            sent.append(x_copies[k, d])
    high = rows // row_blocks
    wide = cols // col_blocks
    base_copy.wait()
    g_copies = {}

    def share(m, f, e, hop):
        came = turned(b, -(f - hop[0]), mid) * inner + turned(c, -(e - hop[1]), inner)
        slot = (m * mid + f) * inner + e
        g_copies[m, f, e] = send(
            mg.at[came, m], mg.at[came, m], g_send.at[slot], g_recv.at[slot], group_peer(*hop)
        )
        sent.append(g_copies[m, f, e])

    for m in range(mats):
        vec_copies[m].wait()

        def merge(i, carry):
            these = pl.ds(pl.multiple_of(i * high, 8), high)
            for j in range(col_blocks):
                across = slice(j * wide, (j + 1) * wide)
                total = base_v[m, these, across].astype(F32)
                for t in range(tasks):
                    scale = coefs[m, t] * scale_of(exps, t, m, i, j)
                    total += scale * vec_v[t, m, these, across].astype(F32)
                mg[mine, m, these, across] = total.astype(BF16)
            return carry

        lax.fori_loop(0, row_blocks, merge, 0)
        for f in range(1, mid):
            share(m, f, 0, (f, 0))
        for e in range(1, inner):
            share(m, 0, e, (0, e))

    r_copies = []
    keeps = []

    def spread(k, d):
        a_from = flip(a, d)
        owner = a_from * group + mine
        for f in range(mid):
            for e in range(inner):
                if not (f or e):
                    continue
                to = turned(b, f, mid) * inner + turned(c, e, inner)
                slot = ((k * outer + d) * mid + f) * inner + e
                r_copies.append(
                    send(
                        xin.at[a_from, some(k), pl.ds(pl.multiple_of(to * rows, 128), rows)],
                        rows_out.at[owner, some(k)],
                        r_send.at[slot], r_recv.at[slot], group_peer(f, e),
                    )
                )
        keeps.append(
            fetch(
                xin.at[a_from, some(k), pl.ds(pl.multiple_of(mine * rows, 128), rows)],
                rows_out.at[owner, some(k)],
                keep_sem.at[k * outer + d],
            )
        )

    y_copies = {}

    def pass_on(k):
        for d in turns:
            x_copies[k, d].wait_recv()
            block = xin.at[flip(a, d), some(k), own_cols]
            for s in range(1, n_tensor):
                slot = (k * outer + d) * n_tensor + s
                y_copies[k, d, s] = send(
                    block, block, y_send.at[slot], y_recv.at[slot], tensor_peer(s)
                )
                sent.append(y_copies[k, d, s])

    def share_on(m):
        for f in range(1, mid):
            g_copies[m, f, 0].wait_recv()
            for e in range(1, inner):
                share(m, f, e, (0, e))

    def own_part(m):
        for f in range(mid):
            for e in range(1, inner):
                g_copies[m, f, e].wait_recv()
        total = None
        for g in range(group):
            term = jnp.dot(
                xin[a, :, g * rows:(g + 1) * rows], mg[g, m], preferred_element_type=F32
            )
            total = term if total is None else total + term
        acc[m] = total

    p_copies = {}

    def give(k, m, d, to):
        slot = (d * pieces + k) * mats + m
        p_copies[k, m, d] = send(
            pout.at[d, m, some(k)], pin.at[d, m, some(k)],
            p_send.at[slot], p_recv.at[slot], at(flip(a, to), b, c),
        )
        sent.append(p_copies[k, m, d])

    def parts(k, m):
        if m == 0:
            for d in turns:
                for s in range(1, n_tensor):
                    y_copies[k, d, s].wait_recv()
        if not turns:
            return
        total = None
        for g in range(group):
            left = jnp.concatenate(
                [xin[flip(a, d), some(k), g * rows:(g + 1) * rows] for d in turns], axis=0
            )
            term = jnp.dot(left, mg[g, m], preferred_element_type=F32)
            total = term if total is None else total + term
        for n, d in enumerate(turns):
            mine_part = total[n * piece:(n + 1) * piece]
            if d == 2:
                hold[m, some(k)] = mine_part
            else:
                pout[d, m, some(k)] = mine_part.astype(BF16)
                give(k, m, d, 1)

    def combine(k, m):
        if 2 not in turns:
            return
        p_copies[k, m, 3].wait_recv()
        pout[2, m, some(k)] = (hold[m, some(k)] + pin[3, m, some(k)].astype(F32)).astype(BF16)
        give(k, m, 2, 2)

    last = pieces - 1
    pass_on(0)
    own_copy.wait()
    for k in range(pieces):
        spread(k, 0)
    share_on(0)
    for k in range(1, last):
        pass_on(k)
    own_part(0)
    for k in range(last):
        parts(k, 0)
        if k:
            combine(k - 1, 0)
        for d in turns:
            spread(k, d)
    share_on(1)
    if last:
        pass_on(last)
        combine(last - 1, 0)
    parts(last, 0)
    own_part(1)
    parts(0, 1)
    combine(last, 0)
    for k in range(1, pieces):
        parts(k, 1)
        combine(k - 1, 1)
    combine(last, 1)
    for d in turns:
        spread(last, d)
    for m in range(mats):
        for k in range(pieces):
            total = acc[m, some(k)]
            for d in turns:
                if d < 3:
                    p_copies[k, m, d].wait_recv()
                    total = total + pin[d, m, some(k)].astype(F32)
            kv_out[m, some(k)] = total.astype(BF16)
    return sent + r_copies, r_copies, keeps


def attend_stage(
    n_tensor, queries, kv, att_out, dkv_out, probs, logs, expos, sums, s_send, s_recv
):
    task = lax.axis_index("task")
    y = lax.axis_index("tensor")
    tokens = queries.shape[0]
    heads = kv.shape[2] // HEAD
    inverse = HEAD ** (-0.5)
    peers = [{"task": task, "tensor": turned(y, s, n_tensor)} for s in range(1, n_tensor)]
    key_at = lax.broadcasted_iota(jnp.int32, (tokens, GROUP * tokens), 0)
    query_at = lax.rem(lax.broadcasted_iota(jnp.int32, (tokens, GROUP * tokens), 1), tokens)
    causal = key_at <= query_at

    def stacked(h):
        return jnp.concatenate(
            [queries[:, (h * GROUP + r) * HEAD:(h * GROUP + r + 1) * HEAD] for r in range(GROUP)],
            axis=0,
        )

    total = jnp.zeros((tokens, HEAD), F32)
    moment = jnp.zeros((tokens, HEAD), F32)
    for h in range(heads):
        cut = slice(h * HEAD, (h + 1) * HEAD)
        scores = lax.dot_general(
            kv[0, :, cut], stacked(h), (((1,), (1,)), ((), ())), preferred_element_type=F32
        ) * inverse
        scores = jnp.where(causal, scores, masked_value)
        weight = jnp.exp(scores - jnp.max(scores, axis=0, keepdims=True))
        prob = weight * (1.0 / jnp.sum(weight, axis=0, keepdims=True))
        probs[h] = prob
        att = lax.dot_general(
            prob.astype(BF16), kv[1, :, cut], (((0,), (0,)), ((), ())), preferred_element_type=F32
        ).astype(BF16)
        logits = capping * jnp.tanh(sharpen * att.astype(F32) / capping)
        expo = jnp.exp(logits)
        logs[h] = logits
        expos[h] = expo
        scaled = expo * logits
        for r in range(GROUP):
            here = slice(r * tokens, (r + 1) * tokens)
            att_out[:, (h * GROUP + r) * HEAD:(h * GROUP + r + 1) * HEAD] = att[here]
            total += expo[here]
            moment += scaled[here]
    sums[y] = jnp.concatenate(
        [
            jnp.sum(total.T, axis=0, keepdims=True),
            jnp.sum(moment.T, axis=0, keepdims=True),
            jnp.zeros((6, tokens), F32),
        ],
        axis=0,
    )
    copies = [
        send(sums.at[y], sums.at[y], s_send.at[s], s_recv.at[s], peer)
        for s, peer in enumerate(peers)
    ]
    for copy in copies:
        copy.wait_recv()
    whole = sums[0]
    for s in range(1, n_tensor):
        whole = whole + sums[s]
    over = 1.0 / whole[0:1]
    average = whole[1:2] * over
    entropy = jnp.sum(jnp.log(whole[0:1]) - average)
    over_col = jnp.broadcast_to(over, (HEAD, tokens)).T
    average_col = jnp.broadcast_to(average, (HEAD, tokens)).T
    over_all = jnp.concatenate([over_col] * GROUP, axis=0)
    average_all = jnp.concatenate([average_col] * GROUP, axis=0)
    for h in range(heads):
        cut = slice(h * HEAD, (h + 1) * HEAD)
        logits = logs[h]
        slope = sharpen * (1.0 - (logits / capping) ** 2)
        d_out = (slope * (-(expos[h] * over_all) * (logits - average_all))).astype(BF16)
        prob = probs[h]
        d_probs = lax.dot_general(
            kv[1, :, cut], d_out, (((1,), (1,)), ((), ())), preferred_element_type=F32
        )
        d_scores = (
            prob * (d_probs - jnp.sum(prob * d_probs, axis=0, keepdims=True))
        ).astype(BF16)
        d_keys = jnp.dot(d_scores, stacked(h), preferred_element_type=F32) * inverse
        d_values = jnp.dot(prob.astype(BF16), d_out, preferred_element_type=F32)
        dkv_out[0, :, cut] = d_keys.astype(BF16)
        dkv_out[1, :, cut] = d_values.astype(BF16)
    return copies, entropy


def reduce_stage(
    dims, n_tensor, task_peers, tensor_peers, rows_ready, entropy,
    dkv, exps, grad_out, mean_out,
    got, rows_v, vec_v, grads, held, held_t,
    g_send, g_recv, t_send, t_recv, y_send, y_recv,
):
    outer, mid, inner = dims
    n_task = outer * mid * inner
    task, a, b, c = place(dims)
    y = lax.axis_index("tensor")
    tasks, mats, rows, cols = vec_v.shape
    row_blocks, col_blocks = exps.shape[1:3]
    near = [d for d in (2, 1, 3) if d < outer]
    order = [0] + near

    def to(d, f, e):
        spot = index_of(dims, flip(a, d), turned(b, f, mid), turned(c, e, inner))
        return {"task": spot, "tensor": y}

    def source(d, f, e):
        return index_of(dims, flip(a, d), turned(b, -f, mid), turned(c, -e, inner))

    copies = {}

    def forward(m, held_at, hop):
        where = source(*held_at)
        slot = tuple(p + q for p, q in zip(held_at, hop))
        flat = ((m * outer + slot[0]) * mid + slot[1]) * inner + slot[2]
        copies[m, slot] = send(
            got.at[m, where] if any(held_at) else dkv.at[m],
            got.at[m, where],
            g_send.at[flat], g_recv.at[flat], to(*hop),
        )

    def take(m, slot):
        if any(slot):
            copies[m, slot].wait_recv()
        d, f, e = slot
        if not e:
            if d and not f:
                for step in range(1, mid):
                    forward(m, slot, (0, step, 0))
            for step in range(1, inner):
                forward(m, slot, (0, 0, step))
        where = source(*slot)
        block = got[m, where] if any(slot) else dkv[m]
        term = lax.dot_general(
            rows_v[where], block, (((0,), (0,)), ((), ())), preferred_element_type=F32
        )
        if any(slot):
            grads[m] += term
        else:
            grads[m] = term

    for m in range(mats):
        for d in near:
            forward(m, (0, 0, 0), (d, 0, 0))
        for step in range(1, mid):
            forward(m, (0, 0, 0), (0, step, 0))
    high = rows // row_blocks
    wide = cols // col_blocks

    def contracted(m):
        def contract(i, carry):
            these = pl.ds(pl.multiple_of(i * high, 8), high)
            carry = list(carry)
            for j in range(col_blocks):
                across = slice(j * wide, (j + 1) * wide)
                grad = grads[m, these, across]
                for t in range(tasks):
                    term = grad * vec_v[t, m, these, across].astype(F32)
                    term = jnp.sum(term.reshape(high // 8, 8, wide), axis=0)
                    carry[t] = carry[t] + scale_of(exps, t, m, i, j) * term
            return tuple(carry)

        start = tuple(jnp.zeros((8, wide), F32) for _ in range(tasks))
        return lax.fori_loop(0, row_blocks, contract, start)

    rows_ready()
    lines = []
    for step in range(mats * outer + 2):
        if step > outer and (step - 2) % outer == 0:
            lines.append(contracted((step - 2) // outer - 1))
        slots = []
        if step < mats * outer:
            slots.append((step, 0, 0))
        if 1 <= step <= mats * outer:
            slots += [(step - 1, f, 0) for f in range(1, mid)]
            slots += [(step - 1, 0, e) for e in range(1, inner)]
        if step >= 2:
            slots += [(step - 2, f, e) for f in range(1, mid) for e in range(1, inner)]
        for at_step, f, e in slots:
            take(at_step // outer, (order[at_step % outer], f, e))
    while len(lines) < mats:
        lines.append(contracted(len(lines)))
    parts = [
        jnp.sum(lines[m][t], axis=0, keepdims=True) for t in range(tasks) for m in range(mats)
    ]
    entropy = jnp.broadcast_to(entropy / (n_tensor * wide), (1, wide))
    pad = -(len(parts) + 1) % 8
    stack = jnp.concatenate(parts + [entropy, jnp.zeros((pad, wide), F32)], axis=0)
    column = jnp.sum(stack, axis=1, keepdims=True)
    shape = (stack.shape[0], held.shape[2])
    along = lax.broadcasted_iota(jnp.int32, shape, 0) == lax.broadcasted_iota(jnp.int32, shape, 1)
    line = jnp.sum(jnp.where(along, column, 0.0), axis=0, keepdims=True)
    held[task] = jnp.broadcast_to(line, held.shape[1:])
    last = [
        send(held.at[task], held.at[task], t_send.at[s], t_recv.at[s], peer)
        for s, peer in enumerate(task_peers)
    ]
    for copy in last:
        copy.wait_recv()
    total = held[0]
    for k in range(1, n_task):
        total = total + held[k]
    held_t[y] = total
    more = [
        send(held_t.at[y], held_t.at[y], y_send.at[s], y_recv.at[s], peer)
        for s, peer in enumerate(tensor_peers)
    ]
    for copy in more:
        copy.wait_recv()
    total = held_t[0]
    for k in range(1, n_tensor):
        total = total + held_t[k]
    tokens = rows_v.shape[1]
    mean_out[...] = total[0:1, tasks * mats:tasks * mats + 1] * (1.0 / (tokens * n_task))
    wide_line = jnp.broadcast_to(total[0:1], (tasks, total.shape[1]))
    spot = lax.broadcasted_iota(jnp.int32, wide_line.shape, 1)
    task_at = lax.broadcasted_iota(jnp.int32, wide_line.shape, 0)
    grid = (mats, total.shape[1])
    mat_at = lax.broadcasted_iota(jnp.int32, grid, 0)
    result = jnp.zeros(grid, F32)
    for m in range(mats):
        column = jnp.sum(jnp.where(spot == mats * task_at + m, wide_line, 0.0), axis=1, keepdims=True)
        row = jnp.sum(jnp.where(spot == task_at, column, 0.0), axis=0, keepdims=True)
        result = jnp.where(mat_at == m, row, result)
    grad_out[...] = result[:, :tasks]
    return list(copies.values()) + last + more


def whole_kernel(
    dims, n_tensor, pieces,
    inputs, queries, vectors, base, exps, coefs,
    att, mean_out, grad_out,
    xin, mg, vec_v, base_v, acc, hold, pout, pin, kv, rows_v, dkv, probs, logs, expos, sums,
    got, grads, held, held_t, smem_sem, exps_v, coefs_v,
    local_sem, keep_sem, x_send, x_recv, y_send, y_recv, g_send, g_recv, r_send, r_recv, p_send, p_recv,
    s_send, s_recv, d_send, d_recv, t_send, t_recv, z_send, z_recv,
):
    n_task = dims[0] * dims[1] * dims[2]
    task = lax.axis_index("task")
    y = lax.axis_index("tensor")
    task_peers = [{"task": turned(task, s, n_task), "tensor": y} for s in range(1, n_task)]
    tensor_peers = [{"task": task, "tensor": turned(y, s, n_tensor)} for s in range(1, n_tensor)]

    small = [fetch(exps, exps_v, smem_sem.at[0]), fetch(coefs, coefs_v, smem_sem.at[1])]

    def greet():
        meet(task_peers + tensor_peers)
        for copy in small:
            copy.wait()

    sent, r_copies, keeps = project_stage(
        dims, n_tensor, pieces, inputs, vectors, base, exps_v, coefs_v, greet, kv, rows_v,
        xin, mg, vec_v, base_v, acc, hold, pout, pin,
        local_sem, keep_sem, x_send, x_recv, y_send, y_recv, g_send, g_recv, r_send, r_recv, p_send, p_recv,
    )
    exchanged, entropy = attend_stage(
        n_tensor, queries, kv, att, dkv, probs, logs, expos, sums, s_send, s_recv
    )

    def rows_ready():
        for copy in keeps:
            copy.wait()
        for copy in r_copies:
            copy.wait_recv()

    more = reduce_stage(
        dims, n_tensor, task_peers, tensor_peers, rows_ready, entropy, dkv, exps_v, grad_out, mean_out,
        got, rows_v, vec_v, grads, held, held_t,
        d_send, d_recv, t_send, t_recv, z_send, z_recv,
    )
    for copy in sent + exchanged + more:
        copy.wait_send()


def local(inputs, queries, task_vectors, base_weights, scale_exps, coefs):
    n_task = lax.axis_size("task")
    n_tensor = lax.axis_size("tensor")
    dims = factors(n_task)
    outer, mid, inner = dims
    group = mid * inner
    tokens = inputs.shape[0]
    tasks, mats, rows, cols = task_vectors.shape
    heads = cols // HEAD
    pieces = math.gcd(tokens // 16, 3)
    hbm = pl.BlockSpec(memory_space=pl.ANY)
    vmem = pl.BlockSpec(memory_space=pltpu.VMEM)
    dma = pltpu.SemaphoreType.DMA

    def pair(count):
        return [dma((count,)), dma((count,))]

    attended, mean_entropy, coef_grad = pl.pallas_call(
        functools.partial(whole_kernel, dims, n_tensor, pieces),
        out_shape=(
            jax.ShapeDtypeStruct(queries.shape, BF16),
            jax.ShapeDtypeStruct((1, 1), F32),
            jax.ShapeDtypeStruct((mats, tasks), F32),
        ),
        in_specs=[hbm, vmem, hbm, hbm, hbm, hbm],
        out_specs=(vmem, vmem, vmem),
        scratch_shapes=[
            pltpu.VMEM((outer, tokens, group * rows), BF16),
            pltpu.VMEM((group, mats, rows, cols), BF16),
            pltpu.VMEM(task_vectors.shape, BF16),
            pltpu.VMEM(base_weights.shape, BF16),
            pltpu.VMEM((mats, tokens, cols), F32),
            pltpu.VMEM((mats, tokens, cols), F32),
            pltpu.VMEM((outer, mats, tokens, cols), BF16),
            pltpu.VMEM((outer, mats, tokens, cols), BF16),
            pltpu.VMEM((mats, tokens, cols), BF16),
            pltpu.VMEM((n_task, tokens, rows), BF16),
            pltpu.VMEM((mats, tokens, cols), BF16),
            pltpu.VMEM((heads, tokens, GROUP * tokens), F32),
            pltpu.VMEM((heads, GROUP * tokens, HEAD), F32),
            pltpu.VMEM((heads, GROUP * tokens, HEAD), F32),
            pltpu.VMEM((n_tensor, 8, tokens), F32),
            pltpu.VMEM((mats, n_task, tokens, cols), BF16),
            pltpu.VMEM((mats, rows, cols), F32),
            pltpu.VMEM((n_task, 8, 128), F32),
            pltpu.VMEM((n_tensor, 8, 128), F32),
            dma((2,)),
            pltpu.SMEM((mats, *scale_exps.shape[2:], tasks), jnp.int32), pltpu.SMEM((mats, tasks), F32),
            dma((2 + mats,)), dma((pieces * outer,)),
            *pair(outer * pieces),
            *pair(pieces * outer * n_tensor),
            *pair(mats * group),
            *pair(pieces * n_task),
            *pair(outer * pieces * mats),
            *pair(n_tensor),
            *pair(mats * n_task),
            *pair(n_task),
            *pair(n_tensor),
        ],
        compiler_params=pltpu.CompilerParams(
            collective_id=0, has_side_effects=True, vmem_limit_bytes=VMEM_BYTES
        ),
        name="whole",
    )(inputs, queries, task_vectors, base_weights, scale_exps.transpose(1, 2, 3, 0), coefs.T)
    return (attended, mean_entropy[0, 0], coef_grad.T)


def solution(mesh):
    return jax.shard_map(
        local,
        mesh=mesh,
        in_specs=(
            P("task", None),
            P("task", "tensor"),
            P(None, None, "task", "tensor"),
            P(None, "task", "tensor"),
            P(None, None, "task", "tensor"),
            P(),
        ),
        out_specs=(P("task", "tensor"), P(), P()),
        check_vma=False,
    )
```

profile of v0, /device:TPU:0, one launch (start us, length us, event | category | flops | bytes accessed | tf_op | source)
XLA Modules:
  0.0 143.5 jit_solution(436938053842634852)
XLA Ops:
  0.6 137.7 %whole.1 = (bf16[192,2048]{1,0:T(8,128)(2,1)}, f32[1,1]{1,0:T(1,128)}, f32[2,8]{1,0:T(2,128)}) custom-call(bf16[192,8192]{1,0:T(8,128)(2,1)} %inputs.1, bf16[192,2048]{1,0:T(8,128)(2,1)} %queries.1, bf16[8,2,512,512]{3,2,1,0:T(8,128)(2,1)} %vectors.1, bf16[2,512,512]{2,1,0:T(8,128)(2,1)} %base.1, s32[2,4,4,8]{3,2,1,0:T(4,128)} %bitcast.4, f32[2,8]{1,0:T(2,128)} %bitcast.6), custom_call_target="tpu_custom_call" | custom-call | tf_op jit(solution)/shard_map/whole/pallas_call | solution.py:599
  138.4 2.1 %copy.12 = bf16[192,2048]{1,0:T(8,128)(2,1)} copy(bf16[192,2048]{1,0:T(8,128)(2,1)} %get-tuple-element.12) | data formatting | bytes 1572864
  141.1 1.2 copy.14
where the time goes:
time: 144 us; the launch traced here: 143 us
  Pallas kernels  138 us (96%)
  local copies, waits for them, and re-layouts  3.32 us (2%)
  between operations  2.41 us (2%)
    pallas_call x1, Pallas kernels, local(): pl.pallas_call(functools.partial(whole_kernel, dims, n_tensor, pieces), o...  138 us
    unnamed x2, local copies, waits for them, and re-layouts  3.32 us

commit v1 on v0

--- a/solution.py
+++ b/solution.py
@@ -50,6 +50,35 @@
 
 def scale_of(exps, t, m, i, j):
     return lax.shift_left(jnp.int32(1), exps[m, i, j, t] + 3).astype(F32) * 0.125
+
+
+def chosen(table, value):
+    total = 0
+    for n, entry in enumerate(table):
+        if not entry:
+            continue
+        term, bit = entry, 1
+        while bit < len(table):
+            digit = lax.rem(value // bit, 2)
+            term = term * (digit if n & bit else 1 - digit)
+            bit *= 2
+        total = total + term
+    return jnp.int32(total) if isinstance(total, int) else total
+
+
+def line_order(outer):
+    sources = [sorted((s for s in range(outer) if s != v), key=lambda s: abs(s - v)) for v in range(outer)]
+    after = [[v + 1 if s < v else v - 1 for s in sources[v]] for v in range(outer)]
+    steps = []
+    for k in range(outer - 1):
+        steps.append(
+            (
+                [sources[v][k] for v in range(outer)],
+                [max(0, min(outer - 1, after[v][k])) for v in range(outer)],
+                [int(0 <= after[v][k] < outer) for v in range(outer)],
+            )
+        )
+    return steps
 
 
 def index_of(dims, a, b, c):
@@ -84,7 +113,7 @@
 
 
 def project_stage(
-    dims, n_tensor, pieces,
+    dims, n_tensor, pieces, bunch,
     inputs, vectors, base, exps, coefs, greet,
     kv_out, rows_out,
     xin, mg, vec_v, base_v, acc, hold, pout, pin,
@@ -114,6 +143,9 @@
 
     def some(k):
         return slice(k * piece, (k + 1) * piece)
+
+    def bunch_of(k):
+        return slice(k * piece * bunch, (k + 1) * piece * bunch)
 
     base_copy = fetch(base, base_v, local_sem.at[0])
     vec_copies = [
@@ -183,15 +215,15 @@
                 slot = ((k * outer + d) * mid + f) * inner + e
                 r_copies.append(
                     send(
-                        xin.at[a_from, some(k), pl.ds(pl.multiple_of(to * rows, 128), rows)],
-                        rows_out.at[owner, some(k)],
+                        xin.at[a_from, bunch_of(k), pl.ds(pl.multiple_of(to * rows, 128), rows)],
+                        rows_out.at[owner, bunch_of(k)],
                         r_send.at[slot], r_recv.at[slot], group_peer(f, e),
                     )
                 )
         keeps.append(
             fetch(
-                xin.at[a_from, some(k), pl.ds(pl.multiple_of(mine * rows, 128), rows)],
-                rows_out.at[owner, some(k)],
+                xin.at[a_from, bunch_of(k), pl.ds(pl.multiple_of(mine * rows, 128), rows)],
+                rows_out.at[owner, bunch_of(k)],
                 keep_sem.at[k * outer + d],
             )
         )
@@ -267,35 +299,8 @@
         give(k, m, 2, 2)
 
     last = pieces - 1
-    pass_on(0)
-    own_copy.wait()
-    for k in range(pieces):
-        spread(k, 0)
-    share_on(0)
-    for k in range(1, last):
-        pass_on(k)
-    own_part(0)
-    for k in range(last):
-        parts(k, 0)
-        if k:
-            combine(k - 1, 0)
-        for d in turns:
-            spread(k, d)
-    share_on(1)
-    if last:
-        pass_on(last)
-        combine(last - 1, 0)
-    parts(last, 0)
-    own_part(1)
-    parts(0, 1)
-    combine(last, 0)
-    for k in range(1, pieces):
-        parts(k, 1)
-        combine(k - 1, 1)
-    combine(last, 1)
-    for d in turns:
-        spread(last, d)
-    for m in range(mats):
+
+    def finish(m):
         for k in range(pieces):
             total = acc[m, some(k)]
             for d in turns:
@@ -303,11 +308,72 @@
                     p_copies[k, m, d].wait_recv()
                     total = total + pin[d, m, some(k)].astype(F32)
             kv_out[m, some(k)] = total.astype(BF16)
-    return sent + r_copies, r_copies, keeps
+
+    done = {m: 0 for m in range(mats)}
+    mixed = {m: 0 for m in range(mats)}
+    spread_done = [0]
+
+    def parts_to(m, count):
+        while done[m] < min(count, pieces):
+            parts(done[m], m)
+            done[m] += 1
+            while m == 0 and (spread_done[0] + 1) * bunch <= done[0]:
+                for d in turns:
+                    spread(spread_done[0], d)
+                spread_done[0] += 1
+
+    def combine_to(m, count):
+        while mixed[m] < min(count, pieces):
+            combine(mixed[m], m)
+            mixed[m] += 1
+
+    pass_on(0)
+    own_copy.wait()
+    for k in range(pieces // bunch):
+        spread(k, 0)
+    for k in range(1, pieces):
+        if k == 2:
+            share_on(0)
+        pass_on(k)
+        if k == 2:
+            own_part(0)
+        if k >= 2:
+            parts_to(0, k)
+        if k == 3:
+            share_on(1)
+            own_part(1)
+        if k >= 4:
+            parts_to(1, 2 * (k - 3))
+        if k == 5:
+            combine_to(0, 3)
+    if pieces <= 2:
+        share_on(0)
+        own_part(0)
+    parts_to(0, pieces)
+    if pieces <= 3:
+        share_on(1)
+        own_part(1)
+    combine_to(0, 4)
+    parts_to(1, pieces)
+    combine_to(0, pieces)
+
+    def keys_ready():
+        combine_to(1, pieces // 2)
+        finish(0)
+
+    def between(h, heads):
+        combine_to(1, pieces // 2 + -(-(h + 1) * (pieces - pieces // 2) // heads))
+
+    def values_ready():
+        combine_to(1, pieces)
+        finish(1)
+
+    return sent, r_copies, keeps, keys_ready, between, values_ready
 
 
 def attend_stage(
-    n_tensor, queries, kv, att_out, dkv_out, probs, logs, expos, sums, s_send, s_recv
+    n_tensor, queries, kv, att_out, dkv_out, probs, logs, expos, outs, sums, s_send, s_recv,
+    keys_ready, between, values_ready, att_done, dkv_done,
 ):
     task = lax.axis_index("task")
     y = lax.axis_index("tensor")
@@ -325,8 +391,7 @@
             axis=0,
         )
 
-    total = jnp.zeros((tokens, HEAD), F32)
-    moment = jnp.zeros((tokens, HEAD), F32)
+    keys_ready()
     for h in range(heads):
         cut = slice(h * HEAD, (h + 1) * HEAD)
         scores = lax.dot_general(
@@ -334,10 +399,15 @@
         ) * inverse
         scores = jnp.where(causal, scores, masked_value)
         weight = jnp.exp(scores - jnp.max(scores, axis=0, keepdims=True))
-        prob = weight * (1.0 / jnp.sum(weight, axis=0, keepdims=True))
-        probs[h] = prob
+        probs[h] = weight * (1.0 / jnp.sum(weight, axis=0, keepdims=True))
+        between(h, heads)
+    values_ready()
+    total = jnp.zeros((tokens, HEAD), F32)
+    moment = jnp.zeros((tokens, HEAD), F32)
+    for h in range(heads):
+        cut = slice(h * HEAD, (h + 1) * HEAD)
         att = lax.dot_general(
-            prob.astype(BF16), kv[1, :, cut], (((0,), (0,)), ((), ())), preferred_element_type=F32
+            probs[h].astype(BF16), kv[1, :, cut], (((0,), (0,)), ((), ())), preferred_element_type=F32
         ).astype(BF16)
         logits = capping * jnp.tanh(sharpen * att.astype(F32) / capping)
         expo = jnp.exp(logits)
@@ -361,6 +431,7 @@
         send(sums.at[y], sums.at[y], s_send.at[s], s_recv.at[s], peer)
         for s, peer in enumerate(peers)
     ]
+    att_done()
     for copy in copies:
         copy.wait_recv()
     whole = sums[0]
@@ -378,25 +449,125 @@
         logits = logs[h]
         slope = sharpen * (1.0 - (logits / capping) ** 2)
         d_out = (slope * (-(expos[h] * over_all) * (logits - average_all))).astype(BF16)
+        outs[h] = d_out
+        d_values = jnp.dot(probs[h].astype(BF16), d_out, preferred_element_type=F32)
+        dkv_out[1, :, cut] = d_values.astype(BF16)
+    dkv_done(1)
+    for h in range(heads):
+        cut = slice(h * HEAD, (h + 1) * HEAD)
         prob = probs[h]
         d_probs = lax.dot_general(
-            kv[1, :, cut], d_out, (((1,), (1,)), ((), ())), preferred_element_type=F32
+            kv[1, :, cut], outs[h], (((1,), (1,)), ((), ())), preferred_element_type=F32
         )
         d_scores = (
             prob * (d_probs - jnp.sum(prob * d_probs, axis=0, keepdims=True))
         ).astype(BF16)
         d_keys = jnp.dot(d_scores, stacked(h), preferred_element_type=F32) * inverse
-        d_values = jnp.dot(prob.astype(BF16), d_out, preferred_element_type=F32)
         dkv_out[0, :, cut] = d_keys.astype(BF16)
-        dkv_out[1, :, cut] = d_values.astype(BF16)
+    dkv_done(0)
     return copies, entropy
 
 
+def spread_plan(dims, mats, dkv, got, g_send, g_recv, z_send, z_recv):
+    outer, mid, inner = dims
+    task, a, b, c = place(dims)
+    y = lax.axis_index("tensor")
+    steps = line_order(outer)
+    planes = [a] + [chosen(source, a) for source, _, _ in steps]
+    group = mid * inner
+    started = []
+    guarded = []
+
+    def spot(plane, f, e):
+        return index_of(dims, plane, turned(b, f, mid), turned(c, e, inner))
+
+    def device(plane, f, e):
+        return {"task": spot(plane, f, e), "tensor": y}
+
+    def along(m, plane, target, slot):
+        source = dkv.at[m] if plane is a else got.at[m, spot(plane, 0, 0)]
+        return pltpu.make_async_remote_copy(
+            src_ref=source,
+            dst_ref=got.at[m, spot(plane, 0, 0)],
+            send_sem=z_send.at[m * (outer + 1) + slot],
+            recv_sem=z_recv.at[m * outer + plane],
+            device_id=device(target, 0, 0),
+            device_id_type=MESH,
+        )
+
+    def guard(copy, valid):
+        @pl.when(valid == 1)
+        def _():
+            copy.start()
+
+        guarded.append((copy, valid))
+
+    copies = {}
+
+    def forward(m, k, held_at, hop):
+        where = index_of(
+            dims, planes[k], turned(b, -held_at[0], mid), turned(c, -held_at[1], inner)
+        )
+        slot = (k, held_at[0] + hop[0], held_at[1] + hop[1])
+        flat = ((m * outer + k) * mid + slot[1]) * inner + slot[2]
+        own = k == 0 and held_at == (0, 0)
+        copies[m, slot] = send(
+            dkv.at[m] if own else got.at[m, where],
+            got.at[m, where],
+            g_send.at[flat], g_recv.at[flat], device(a, *hop),
+        )
+        started.append(copies[m, slot])
+
+    def sent_own(m):
+        for k in range(1, 2):
+            if outer > 1:
+                for step, slot in ((1, outer - 1), (-1, outer)):
+                    valid = [int(0 <= v + step < outer) for v in range(outer)]
+                    target = [max(0, min(outer - 1, v + step)) for v in range(outer)]
+                    guard(along(m, a, chosen(target, a), slot), chosen(valid, a))
+        for f in range(1, mid):
+            forward(m, 0, (0, 0), (f, 0))
+        for e in range(1, inner):
+            forward(m, 0, (0, 0), (0, e))
+
+    def arrive(m, k):
+        plane = planes[k]
+        _, target, valid = steps[k - 1]
+        copy = along(m, plane, chosen(target, a), k - 1)
+        copy.wait_recv()
+        guard(copy, chosen(valid, a))
+        for f in range(1, mid):
+            forward(m, k, (0, 0), (f, 0))
+        for e in range(1, inner):
+            forward(m, k, (0, 0), (0, e))
+
+    def across(m, k, f):
+        copies[m, (k, f, 0)].wait_recv()
+        for e in range(1, inner):
+            forward(m, k, (f, 0), (0, e))
+
+    def core(m, k, f, e):
+        copies[m, (k, f, e)].wait_recv()
+
+    def source(k, f, e):
+        return index_of(dims, planes[k], turned(b, -f, mid), turned(c, -e, inner))
+
+    def drain():
+        for copy in started:
+            copy.wait_send()
+        for copy, valid in guarded:
+            @pl.when(valid == 1)
+            def _():
+                copy.wait_send()
+
+    return sent_own, arrive, across, core, source, drain
+
+
 def reduce_stage(
-    dims, n_tensor, task_peers, tensor_peers, rows_ready, entropy,
+    dims, n_tensor, task_peers, tensor_peers, rows_ready, entropy, plan,
     dkv, exps, grad_out, mean_out,
     got, rows_v, vec_v, grads, held, held_t,
-    g_send, g_recv, t_send, t_recv, y_send, y_recv,
+    t_send, t_recv, y_send, y_recv,
 ):
     outer, mid, inner = dims
     n_task = outer * mid * inner
@@ -404,53 +575,28 @@
     y = lax.axis_index("tensor")
     tasks, mats, rows, cols = vec_v.shape
     row_blocks, col_blocks = exps.shape[1:3]
-    near = [d for d in (2, 1, 3) if d < outer]
-    order = [0] + near
-
-    def to(d, f, e):
-        spot = index_of(dims, flip(a, d), turned(b, f, mid), turned(c, e, inner))
-        return {"task": spot, "tensor": y}
-
-    def source(d, f, e):
-        return index_of(dims, flip(a, d), turned(b, -f, mid), turned(c, -e, inner))
-
-    copies = {}
-
-    def forward(m, held_at, hop):
-        where = source(*held_at)
-        slot = tuple(p + q for p, q in zip(held_at, hop))
-        flat = ((m * outer + slot[0]) * mid + slot[1]) * inner + slot[2]
-        copies[m, slot] = send(
-            got.at[m, where] if any(held_at) else dkv.at[m],
-            got.at[m, where],
-            g_send.at[flat], g_recv.at[flat], to(*hop),
-        )
-
-    def take(m, slot):
-        if any(slot):
-            copies[m, slot].wait_recv()
-        d, f, e = slot
-        if not e:
-            if d and not f:
-                for step in range(1, mid):
-                    forward(m, slot, (0, step, 0))
-            for step in range(1, inner):
-                forward(m, slot, (0, 0, step))
-        where = source(*slot)
-        block = got[m, where] if any(slot) else dkv[m]
+    _, arrive, across, core, source, drain = plan
+    fresh = set()
+
+    def take(m, k, f, e):
+        own = not (k or f or e)
+        if k and not (f or e):
+            arrive(m, k)
+        elif f and not e:
+            across(m, k, f)
+        elif e:
+            core(m, k, f, e)
+        where = source(k, f, e)
+        block = dkv[m] if own else got[m, where]
         term = lax.dot_general(
             rows_v[where], block, (((0,), (0,)), ((), ())), preferred_element_type=F32
         )
-        if any(slot):
+        if m in fresh:
             grads[m] += term
         else:
             grads[m] = term
-
-    for m in range(mats):
-        for d in near:
-            forward(m, (0, 0, 0), (d, 0, 0))
-        for step in range(1, mid):
-            forward(m, (0, 0, 0), (0, step, 0))
+            fresh.add(m)
+
     high = rows // row_blocks
     wide = cols // col_blocks
 
@@ -471,22 +617,22 @@
         return lax.fori_loop(0, row_blocks, contract, start)
 
     rows_ready()
-    lines = []
-    for step in range(mats * outer + 2):
-        if step > outer and (step - 2) % outer == 0:
-            lines.append(contracted((step - 2) // outer - 1))
+    lines = {}
+    turns = [(k, m) for k in range(outer) for m in reversed(range(mats))]
+    for step in range(len(turns) + 2):
         slots = []
-        if step < mats * outer:
-            slots.append((step, 0, 0))
-        if 1 <= step <= mats * outer:
-            slots += [(step - 1, f, 0) for f in range(1, mid)]
-            slots += [(step - 1, 0, e) for e in range(1, inner)]
+        if step < len(turns):
+            slots.append((turns[step], 0, 0))
+        if 1 <= step <= len(turns):
+            slots += [(turns[step - 1], f, 0) for f in range(1, mid)]
+            slots += [(turns[step - 1], 0, e) for e in range(1, inner)]
         if step >= 2:
-            slots += [(step - 2, f, e) for f in range(1, mid) for e in range(1, inner)]
-        for at_step, f, e in slots:
-            take(at_step // outer, (order[at_step % outer], f, e))
-    while len(lines) < mats:
-        lines.append(contracted(len(lines)))
+            slots += [(turns[step - 2], f, e) for f in range(1, mid) for e in range(1, inner)]
+        for (k, m), f, e in slots:
+            take(m, k, f, e)
+        if step - 2 >= len(turns) - mats:
+            m = turns[step - 2][1]
+            lines[m] = contracted(m)
     parts = [
         jnp.sum(lines[m][t], axis=0, keepdims=True) for t in range(tasks) for m in range(mats)
     ]
@@ -530,17 +676,18 @@
         row = jnp.sum(jnp.where(spot == task_at, column, 0.0), axis=0, keepdims=True)
         result = jnp.where(mat_at == m, row, result)
     grad_out[...] = result[:, :tasks]
-    return list(copies.values()) + last + more
+    drain()
+    return last + more
 
 
 def whole_kernel(
-    dims, n_tensor, pieces,
+    dims, n_tensor, pieces, bunch,
     inputs, queries, vectors, base, exps, coefs,
     att, mean_out, grad_out,
-    xin, mg, vec_v, base_v, acc, hold, pout, pin, kv, rows_v, dkv, probs, logs, expos, sums,
-    got, grads, held, held_t, smem_sem, exps_v, coefs_v,
+    xin, mg, vec_v, base_v, acc, hold, pout, pin, kv, rows_v, dkv, probs, logs, expos, outs, sums,
+    got, grads, held, held_t, q_v, att_v, io_sem, smem_sem, exps_v, coefs_v,
     local_sem, keep_sem, x_send, x_recv, y_send, y_recv, g_send, g_recv, r_send, r_recv, p_send, p_recv,
-    s_send, s_recv, d_send, d_recv, t_send, t_recv, z_send, z_recv,
+    s_send, s_recv, d_send, d_recv, l_send, l_recv, t_send, t_recv, z_send, z_recv,
 ):
     n_task = dims[0] * dims[1] * dims[2]
     task = lax.axis_index("task")
@@ -549,19 +696,28 @@
     tensor_peers = [{"task": task, "tensor": turned(y, s, n_tensor)} for s in range(1, n_tensor)]
 
     small = [fetch(exps, exps_v, smem_sem.at[0]), fetch(coefs, coefs_v, smem_sem.at[1])]
+    waiting = []
 
     def greet():
         meet(task_peers + tensor_peers)
         for copy in small:
             copy.wait()
 
-    sent, r_copies, keeps = project_stage(
-        dims, n_tensor, pieces, inputs, vectors, base, exps_v, coefs_v, greet, kv, rows_v,
+    query_copy = fetch(queries, q_v, io_sem.at[0])
+    sent, r_copies, keeps, keys_ready, between, values_ready = project_stage(
+        dims, n_tensor, pieces, bunch, inputs, vectors, base, exps_v, coefs_v, greet, kv, rows_v,
         xin, mg, vec_v, base_v, acc, hold, pout, pin,
         local_sem, keep_sem, x_send, x_recv, y_send, y_recv, g_send, g_recv, r_send, r_recv, p_send, p_recv,
     )
+    query_copy.wait()
+    plan = spread_plan(dims, kv.shape[0], dkv, got, d_send, d_recv, l_send, l_recv)
+
+    def att_done():
+        waiting.append(fetch(att_v, att, io_sem.at[1]))
+
     exchanged, entropy = attend_stage(
-        n_tensor, queries, kv, att, dkv, probs, logs, expos, sums, s_send, s_recv
+        n_tensor, q_v, kv, att_v, dkv, probs, logs, expos, outs, sums, s_send, s_recv,
+        keys_ready, between, values_ready, att_done, plan[0],
     )
 
     def rows_ready():
@@ -571,12 +727,15 @@
             copy.wait_recv()
 
     more = reduce_stage(
-        dims, n_tensor, task_peers, tensor_peers, rows_ready, entropy, dkv, exps_v, grad_out, mean_out,
+        dims, n_tensor, task_peers, tensor_peers, rows_ready, entropy, plan,
+        dkv, exps_v, grad_out, mean_out,
         got, rows_v, vec_v, grads, held, held_t,
-        d_send, d_recv, t_send, t_recv, z_send, z_recv,
+        t_send, t_recv, z_send, z_recv,
     )
-    for copy in sent + exchanged + more:
+    for copy in sent + r_copies + exchanged + more:
         copy.wait_send()
+    for copy in waiting:
+        copy.wait()
 
 
 def local(inputs, queries, task_vectors, base_weights, scale_exps, coefs):
@@ -588,7 +747,8 @@
     tokens = inputs.shape[0]
     tasks, mats, rows, cols = task_vectors.shape
     heads = cols // HEAD
-    pieces = math.gcd(tokens // 16, 3)
+    pieces = math.gcd(tokens // 16, 6)
+    bunch = math.gcd(pieces, 2)
     hbm = pl.BlockSpec(memory_space=pl.ANY)
     vmem = pl.BlockSpec(memory_space=pltpu.VMEM)
     dma = pltpu.SemaphoreType.DMA
@@ -597,14 +757,14 @@
         return [dma((count,)), dma((count,))]
 
     attended, mean_entropy, coef_grad = pl.pallas_call(
-        functools.partial(whole_kernel, dims, n_tensor, pieces),
+        functools.partial(whole_kernel, dims, n_tensor, pieces, bunch),
         out_shape=(
             jax.ShapeDtypeStruct(queries.shape, BF16),
             jax.ShapeDtypeStruct((1, 1), F32),
             jax.ShapeDtypeStruct((mats, tasks), F32),
         ),
-        in_specs=[hbm, vmem, hbm, hbm, hbm, hbm],
-        out_specs=(vmem, vmem, vmem),
+        in_specs=[hbm] * 6,
+        out_specs=(hbm, vmem, vmem),
         scratch_shapes=[
             pltpu.VMEM((outer, tokens, group * rows), BF16),
             pltpu.VMEM((group, mats, rows, cols), BF16),
@@ -620,21 +780,26 @@
             pltpu.VMEM((heads, tokens, GROUP * tokens), F32),
             pltpu.VMEM((heads, GROUP * tokens, HEAD), F32),
             pltpu.VMEM((heads, GROUP * tokens, HEAD), F32),
+            pltpu.VMEM((heads, GROUP * tokens, HEAD), BF16),
             pltpu.VMEM((n_tensor, 8, tokens), F32),
             pltpu.VMEM((mats, n_task, tokens, cols), BF16),
             pltpu.VMEM((mats, rows, cols), F32),
             pltpu.VMEM((n_task, 8, 128), F32),
             pltpu.VMEM((n_tensor, 8, 128), F32),
+            pltpu.VMEM(queries.shape, BF16),
+            pltpu.VMEM(queries.shape, BF16),
+            dma((2,)),
             dma((2,)),
             pltpu.SMEM((mats, *scale_exps.shape[2:], tasks), jnp.int32), pltpu.SMEM((mats, tasks), F32),
             dma((2 + mats,)), dma((pieces * outer,)),
             *pair(outer * pieces),
             *pair(pieces * outer * n_tensor),
             *pair(mats * group),
-            *pair(pieces * n_task),
+            *pair((pieces // bunch) * n_task),
             *pair(outer * pieces * mats),
             *pair(n_tensor),
             *pair(mats * n_task),
+            dma((mats * (outer + 1),)), dma((mats * outer,)),
             *pair(n_task),
             *pair(n_tensor),
         ],

time: 144 us -> 131 us (0.910)
  Pallas kernels: 138 us -> 126 us
    pallas_call x1, Pallas kernels: 138 us -> 126 us  [local(): pl.pallas_call(functools.partial(whole_kernel, dims, n_tensor, pieces, bu...]
where the time goes in v1:
time: 131 us
  Pallas kernels  126 us (96%)
  local copies, waits for them, and re-layouts  3.32 us (3%)
  between operations  2.41 us (2%)
    pallas_call x1, Pallas kernels, local(): pl.pallas_call(functools.partial(whole_kernel, dims, n_tensor, pieces, bu...  126 us
    unnamed x2, local copies, waits for them, and re-layouts  3.32 us

profile of v1, /device:TPU:0, one launch (start us, length us, event | category | flops | bytes accessed | tf_op | source)
XLA Modules:
  0.0 131.3 jit_solution(8334362702185154815)
XLA Ops:
  0.6 125.5 %whole.1 = (bf16[192,2048]{1,0:T(8,128)(2,1)}, f32[1,1]{1,0:T(1,128)}, f32[2,8]{1,0:T(2,128)}) custom-call(bf16[192,8192]{1,0:T(8,128)(2,1)} %inputs.1, bf16[192,2048]{1,0:T(8,128)(2,1)} %queries.1, bf16[8,2,512,512]{3,2,1,0:T(8,128)(2,1)} %vectors.1, bf16[2,512,512]{2,1,0:T(8,128)(2,1)} %base.1, s32[2,4,4,8]{3,2,1,0:T(4,128)} %bitcast.4, f32[2,8]{1,0:T(2,128)} %bitcast.6), custom_call_target="tpu_custom_call" | custom-call | tf_op jit(solution)/shard_map/whole/pallas_call | solution.py:759
  126.2 2.1 %copy.12 = bf16[192,2048]{1,0:T(8,128)(2,1)} copy(bf16[192,2048]{1,0:T(8,128)(2,1)} %get-tuple-element.12) | data formatting | bytes 1572864
  128.9 1.2 copy.14

commit v2 on v1

--- a/solution.py
+++ b/solution.py
@@ -16,7 +16,7 @@
 masked_value = -1e30
 
 MESH = pl.DeviceIdType.MESH
-VMEM_BYTES = 60 * 1024 * 1024
+VMEM_BYTES = 48 * 1024 * 1024
 F32 = jnp.float32
 BF16 = jnp.bfloat16
 
@@ -67,7 +67,7 @@
 
 
 def line_order(outer):
-    sources = [sorted((s for s in range(outer) if s != v), key=lambda s: abs(s - v)) for v in range(outer)]
+    sources = [sorted((s for s in range(outer) if s != v), key=lambda s: (abs(s - v), s if 2 * v < outer else -s)) for v in range(outer)]
     after = [[v + 1 if s < v else v - 1 for s in sources[v]] for v in range(outer)]
     steps = []
     for k in range(outer - 1):
@@ -104,6 +104,18 @@
     )
     copy.start()
     return copy
+
+
+def sent_all(ref, sem, peer):
+    pltpu.make_async_remote_copy(
+        src_ref=ref, dst_ref=ref, send_sem=sem, recv_sem=sem, device_id=peer, device_id_type=MESH
+    ).wait_send()
+
+
+def came_all(ref, sem, peer):
+    pltpu.make_async_remote_copy(
+        src_ref=ref, dst_ref=ref, send_sem=sem, recv_sem=sem, device_id=peer, device_id_type=MESH
+    ).wait_recv()
 
 
 def fetch(src, dst, sem):
@@ -130,6 +142,7 @@
     piece = tokens // pieces
     span = group * rows
     part = span // n_tensor
+    window = 3
     turns = list(range(outer - 1, 0, -1))
 
     def at(a_, b_, c_):
@@ -155,19 +168,21 @@
         inputs.at[:, pl.ds(pl.multiple_of(a * span, 128), span)], xin.at[a], local_sem.at[1]
     )
     greet()
-    sent = []
     x_copies = {}
     own_cols = pl.ds(pl.multiple_of(y * part, 128), part)
-    for k in range(pieces):
+
+    def hand_out(k):
         for d in turns:
             to = flip(a, d)
             slot = d * pieces + k
             x_copies[k, d] = send(
                 inputs.at[some(k), pl.ds(pl.multiple_of(to * span + y * part, 128), part)],
                 xin.at[a, some(k), own_cols],
-                x_send.at[slot], x_recv.at[slot], at(to, b, c),
+                x_send.at[0], x_recv.at[slot], at(to, b, c),
             )
-            sent.append(x_copies[k, d])
+
+    for k in range(min(window, pieces)):
+        hand_out(k)
     high = rows // row_blocks
     wide = cols // col_blocks
     base_copy.wait()
@@ -177,9 +192,8 @@
         came = turned(b, -(f - hop[0]), mid) * inner + turned(c, -(e - hop[1]), inner)
         slot = (m * mid + f) * inner + e
         g_copies[m, f, e] = send(
-            mg.at[came, m], mg.at[came, m], g_send.at[slot], g_recv.at[slot], group_peer(*hop)
-        )
-        sent.append(g_copies[m, f, e])
+            mg.at[came, m], mg.at[came, m], g_send.at[0], g_recv.at[slot], group_peer(*hop)
+        )
 
     for m in range(mats):
         vec_copies[m].wait()
@@ -201,9 +215,6 @@
         for e in range(1, inner):
             share(m, 0, e, (0, e))
 
-    r_copies = []
-    keeps = []
-
     def spread(k, d):
         a_from = flip(a, d)
         owner = a_from * group + mine
@@ -212,34 +223,26 @@
                 if not (f or e):
                     continue
                 to = turned(b, f, mid) * inner + turned(c, e, inner)
-                slot = ((k * outer + d) * mid + f) * inner + e
-                r_copies.append(
-                    send(
-                        xin.at[a_from, bunch_of(k), pl.ds(pl.multiple_of(to * rows, 128), rows)],
-                        rows_out.at[owner, bunch_of(k)],
-                        r_send.at[slot], r_recv.at[slot], group_peer(f, e),
-                    )
+                send(
+                    xin.at[a_from, bunch_of(k), pl.ds(pl.multiple_of(to * rows, 128), rows)],
+                    rows_out.at[owner, bunch_of(k)],
+                    r_send.at[0], r_recv.at[0], group_peer(f, e),
                 )
-        keeps.append(
-            fetch(
-                xin.at[a_from, bunch_of(k), pl.ds(pl.multiple_of(mine * rows, 128), rows)],
-                rows_out.at[owner, bunch_of(k)],
-                keep_sem.at[k * outer + d],
-            )
-        )
-
-    y_copies = {}
+        fetch(
+            xin.at[a_from, bunch_of(k), pl.ds(pl.multiple_of(mine * rows, 128), rows)],
+            rows_out.at[owner, bunch_of(k)],
+            keep_sem.at[0],
+        )
 
     def pass_on(k):
         for d in turns:
             x_copies[k, d].wait_recv()
+        if k + window < pieces:
+            hand_out(k + window)
+        for d in turns:
             block = xin.at[flip(a, d), some(k), own_cols]
             for s in range(1, n_tensor):
-                slot = (k * outer + d) * n_tensor + s
-                y_copies[k, d, s] = send(
-                    block, block, y_send.at[slot], y_recv.at[slot], tensor_peer(s)
-                )
-                sent.append(y_copies[k, d, s])
+                send(block, block, y_send.at[0], y_recv.at[k], tensor_peer(s))
 
     def share_on(m):
         for f in range(1, mid):
@@ -261,21 +264,20 @@
 
     p_copies = {}
 
+    def p_slot(k, m, d):
+        return m * (pieces + 2) + (k if d == 3 else pieces + d - 1)
+
     def give(k, m, d, to):
-        slot = (d * pieces + k) * mats + m
         p_copies[k, m, d] = send(
             pout.at[d, m, some(k)], pin.at[d, m, some(k)],
-            p_send.at[slot], p_recv.at[slot], at(flip(a, to), b, c),
-        )
-        sent.append(p_copies[k, m, d])
+            p_send.at[0], p_recv.at[p_slot(k, m, d)], at(flip(a, to), b, c),
+        )
 
     def parts(k, m):
-        if m == 0:
-            for d in turns:
-                for s in range(1, n_tensor):
-                    y_copies[k, d, s].wait_recv()
         if not turns:
             return
+        if m == 0 and n_tensor > 1:
+            came_all(xin.at[:len(turns), some(k), :span - part], y_recv.at[k], tensor_peer(1))
         total = None
         for g in range(group):
             left = jnp.concatenate(
@@ -301,13 +303,12 @@
     last = pieces - 1
 
     def finish(m):
-        for k in range(pieces):
-            total = acc[m, some(k)]
-            for d in turns:
-                if d < 3:
-                    p_copies[k, m, d].wait_recv()
-                    total = total + pin[d, m, some(k)].astype(F32)
-            kv_out[m, some(k)] = total.astype(BF16)
+        total = acc[m]
+        for d in turns:
+            if d < 3:
+                came_all(pin.at[d, m], p_recv.at[p_slot(0, m, d)], at(flip(a, d), b, c))
+                total = total + pin[d, m].astype(F32)
+        kv_out[m] = total.astype(BF16)
 
     done = {m: 0 for m in range(mats)}
     mixed = {m: 0 for m in range(mats)}
@@ -327,34 +328,47 @@
             combine(mixed[m], m)
             mixed[m] += 1
 
+    shared = set()
+
+    def shared_up_to(m):
+        for n in range(m + 1):
+            if n not in shared:
+                shared.add(n)
+                share_on(n)
+                own_part(n)
+
     pass_on(0)
     own_copy.wait()
     for k in range(pieces // bunch):
         spread(k, 0)
     for k in range(1, pieces):
+        pass_on(k)
+        if k == 1:
+            shared_up_to(0)
+            parts_to(0, 1)
         if k == 2:
-            share_on(0)
-        pass_on(k)
-        if k == 2:
-            own_part(0)
-        if k >= 2:
-            parts_to(0, k)
+            parts_to(0, 2)
+            shared_up_to(1)
+            parts_to(1, 1)
         if k == 3:
-            share_on(1)
-            own_part(1)
-        if k >= 4:
-            parts_to(1, 2 * (k - 3))
+            parts_to(1, 2)
+        if k == 4:
+            parts_to(0, 3)
+            parts_to(1, 3)
+            combine_to(0, 1)
         if k == 5:
-            combine_to(0, 3)
-    if pieces <= 2:
-        share_on(0)
-        own_part(0)
+            parts_to(0, 4)
+            parts_to(1, 4)
+            combine_to(0, 2)
+    shared_up_to(mats - 1)
+    parts_to(0, pieces - 1)
+    combine_to(0, 3)
+    parts_to(1, pieces - 1)
+    combine_to(0, 4)
     parts_to(0, pieces)
-    if pieces <= 3:
-        share_on(1)
-        own_part(1)
-    combine_to(0, 4)
     parts_to(1, pieces)
+    combine_to(0, 5)
+    combine_to(1, 2)
     combine_to(0, pieces)
 
     def keys_ready():
@@ -368,7 +382,24 @@
         combine_to(1, pieces)
         finish(1)
 
-    return sent, r_copies, keeps, keys_ready, between, values_ready
+    def rows_ready():
+        spread_all = rows_out.at[:outer]
+        pltpu.make_async_copy(spread_all, spread_all, keep_sem.at[0]).wait()
+        if group > 1:
+            came_all(rows_out.at[:outer * (group - 1)], r_recv.at[0], group_peer(0, 1))
+
+    def drain():
+        peer = group_peer(0, 1)
+        if turns:
+            sent_all(xin.at[:len(turns), :, :part], x_send.at[0], peer)
+            sent_all(pout.at[1:1 + len(turns)], p_send.at[0], peer)
+            if n_tensor > 1:
+                sent_all(xin.at[:len(turns), :, :span - part], y_send.at[0], peer)
+        if group > 1:
+            sent_all(mg.at[:group - 1], g_send.at[0], peer)
+            sent_all(rows_out.at[:outer * (group - 1)], r_send.at[0], peer)
+
+    return keys_ready, between, values_ready, rows_ready, drain
 
 
 def attend_stage(
@@ -468,15 +499,20 @@
     return copies, entropy
 
 
-def spread_plan(dims, mats, dkv, got, g_send, g_recv, z_send, z_recv):
+def spread_plan(dims, mats, dkv, got, d_send, d_recv, l_send, l_recv, u_send):
     outer, mid, inner = dims
     task, a, b, c = place(dims)
     y = lax.axis_index("tensor")
     steps = line_order(outer)
     planes = [a] + [chosen(source, a) for source, _, _ in steps]
     group = mid * inner
-    started = []
-    guarded = []
+    up = [int(v + 1 < outer) for v in range(outer)]
+    down = [int(v > 0) for v in range(outer)]
+    above = chosen([min(v + 1, outer - 1) for v in range(outer)], a)
+    below = chosen([max(v - 1, 0) for v in range(outer)], a)
+    inside = chosen([u * d for u, d in zip(up, down)], a)
+    detour = outer == 4 and mid == 2
+    last = 0
 
     def spot(plane, f, e):
         return index_of(dims, plane, turned(b, f, mid), turned(c, e, inner))
@@ -484,13 +520,27 @@
     def device(plane, f, e):
         return {"task": spot(plane, f, e), "tensor": y}
 
-    def along(m, plane, target, slot):
+    def slot_of(m, k, f, e):
+        return ((m * outer + k) * mid + f) * inner + e
+
+    def along(m, plane, target):
         source = dkv.at[m] if plane is a else got.at[m, spot(plane, 0, 0)]
         return pltpu.make_async_remote_copy(
             src_ref=source,
             dst_ref=got.at[m, spot(plane, 0, 0)],
-            send_sem=z_send.at[m * (outer + 1) + slot],
-            recv_sem=z_recv.at[m * outer + plane],
+            send_sem=l_send.at[0],
+            recv_sem=l_recv.at[m * outer + plane],
+            device_id=device(target, 0, 0),
+            device_id_type=MESH,
+        )
+
+    def beside(k, target, k_there):
+        block = got.at[last, spot(planes[k], 1, 0)]
+        return pltpu.make_async_remote_copy(
+            src_ref=block,
+            dst_ref=block,
+            send_sem=u_send.at[0],
+            recv_sem=d_recv.at[slot_of(last, k_there, 1, 0)],
             device_id=device(target, 0, 0),
             device_id_type=MESH,
         )
@@ -500,8 +550,6 @@
         def _():
             copy.start()
 
-        guarded.append((copy, valid))
-
     copies = {}
 
     def forward(m, k, held_at, hop):
@@ -509,31 +557,34 @@
             dims, planes[k], turned(b, -held_at[0], mid), turned(c, -held_at[1], inner)
         )
         slot = (k, held_at[0] + hop[0], held_at[1] + hop[1])
-        flat = ((m * outer + k) * mid + slot[1]) * inner + slot[2]
         own = k == 0 and held_at == (0, 0)
-        copies[m, slot] = send(
-            dkv.at[m] if own else got.at[m, where],
-            got.at[m, where],
-            g_send.at[flat], g_recv.at[flat], device(a, *hop),
-        )
-        started.append(copies[m, slot])
+        around = detour and m == last and k in (1, 3) and hop[0]
+        copy = pltpu.make_async_remote_copy(
+            src_ref=dkv.at[m] if own else got.at[m, where],
+            dst_ref=got.at[m, where],
+            send_sem=u_send.at[0] if around else d_send.at[m if detour else 0],
+            recv_sem=d_recv.at[slot_of(m, *slot)],
+            device_id=device(a, *hop),
+            device_id_type=MESH,
+        )
+        copies[m, slot] = copy
+        if not around:
+            copy.start()
+        elif k == 1:
+            guard(copy, 1 - inside)
 
     def sent_own(m):
-        for k in range(1, 2):
-            if outer > 1:
-                for step, slot in ((1, outer - 1), (-1, outer)):
-                    valid = [int(0 <= v + step < outer) for v in range(outer)]
-                    target = [max(0, min(outer - 1, v + step)) for v in range(outer)]
-                    guard(along(m, a, chosen(target, a), slot), chosen(valid, a))
+        if outer > 1:
+            guard(along(m, a, above), chosen(up, a))
+            guard(along(m, a, below), chosen(down, a))
         for f in range(1, mid):
             forward(m, 0, (0, 0), (f, 0))
         for e in range(1, inner):
             forward(m, 0, (0, 0), (0, e))
 
     def arrive(m, k):
-        plane = planes[k]
         _, target, valid = steps[k - 1]
-        copy = along(m, plane, chosen(target, a), k - 1)
+        copy = along(m, planes[k], chosen(target, a))
         copy.wait_recv()
         guard(copy, chosen(valid, a))
         for f in range(1, mid):
@@ -545,6 +596,12 @@
         copies[m, (k, f, 0)].wait_recv()
         for e in range(1, inner):
             forward(m, k, (f, 0), (0, e))
+        if not detour or m != last:
+            return
+        if k == 0:
+            guard(beside(0, chosen([1, 0, 3, 2], a), 1), 1 - inside)
+        elif k != 2:
+            guard(beside(k, chosen(steps[k - 1][1], a), 3), inside)
 
     def core(m, k, f, e):
         copies[m, (k, f, e)].wait_recv()
@@ -553,21 +610,32 @@
         return index_of(dims, planes[k], turned(b, -f, mid), turned(c, -e, inner))
 
     def drain():
-        for copy in started:
-            copy.wait_send()
-        for copy, valid in guarded:
-            @pl.when(valid == 1)
+        peer = device(a, 0, 1)
+        if group > 1:
+            count = outer * (group - 1)
+            if not detour:
+                sent_all(got.at[:, :count], d_send.at[0], peer)
+            for m in range(mats if detour else 0):
+                kept = count - 2 if m == last else count
+                sent_all(got.at[m, :kept], d_send.at[m], peer)
+        if detour:
+            sent_all(got.at[0, :2], u_send.at[0], peer)
+        if outer > 1:
+            @pl.when(inside == 1)
             def _():
-                copy.wait_send()
+                sent_all(got.at[:, :outer + 1], l_send.at[0], peer)
+
+            @pl.when(inside == 0)
+            def _():
+                sent_all(got.at[:, :1], l_send.at[0], peer)
 
     return sent_own, arrive, across, core, source, drain
 
 
 def reduce_stage(
-    dims, n_tensor, task_peers, tensor_peers, rows_ready, entropy, plan,
+    dims, n_tensor, groups, rows_ready, entropy, plan,
     dkv, exps, grad_out, mean_out,
-    got, rows_v, vec_v, grads, held, held_t,
-    t_send, t_recv, y_send, y_recv,
+    got, rows_v, vec_v, grads, helds, t_send, t_recv,
 ):
     outer, mid, inner = dims
     n_task = outer * mid * inner
@@ -640,29 +708,18 @@
     pad = -(len(parts) + 1) % 8
     stack = jnp.concatenate(parts + [entropy, jnp.zeros((pad, wide), F32)], axis=0)
     column = jnp.sum(stack, axis=1, keepdims=True)
-    shape = (stack.shape[0], held.shape[2])
+    shape = (stack.shape[0], helds[0].shape[2])
     along = lax.broadcasted_iota(jnp.int32, shape, 0) == lax.broadcasted_iota(jnp.int32, shape, 1)
-    line = jnp.sum(jnp.where(along, column, 0.0), axis=0, keepdims=True)
-    held[task] = jnp.broadcast_to(line, held.shape[1:])
-    last = [
-        send(held.at[task], held.at[task], t_send.at[s], t_recv.at[s], peer)
-        for s, peer in enumerate(task_peers)
-    ]
-    for copy in last:
-        copy.wait_recv()
-    total = held[0]
-    for k in range(1, n_task):
-        total = total + held[k]
-    held_t[y] = total
-    more = [
-        send(held_t.at[y], held_t.at[y], y_send.at[s], y_recv.at[s], peer)
-        for s, peer in enumerate(tensor_peers)
-    ]
-    for copy in more:
-        copy.wait_recv()
-    total = held_t[0]
-    for k in range(1, n_tensor):
-        total = total + held_t[k]
+    total = jnp.sum(jnp.where(along, column, 0.0), axis=0, keepdims=True)
+    for n, (held, (slot, peers)) in enumerate(zip(helds, groups)):
+        held[slot] = total
+        for peer in peers:
+            send(held.at[slot], held.at[slot], t_send.at[n], t_recv.at[n], peer)
+        if peers:
+            came_all(held.at[:len(peers)], t_recv.at[n], peers[0])
+        total = held[0]
+        for k in range(1, len(peers) + 1):
+            total = total + held[k]
     tokens = rows_v.shape[1]
     mean_out[...] = total[0:1, tasks * mats:tasks * mats + 1] * (1.0 / (tokens * n_task))
     wide_line = jnp.broadcast_to(total[0:1], (tasks, total.shape[1]))
@@ -677,7 +734,9 @@
         result = jnp.where(mat_at == m, row, result)
     grad_out[...] = result[:, :tasks]
     drain()
-    return last + more
+    for n, (held, (slot, peers)) in enumerate(zip(helds, groups)):
+        if peers:
+            sent_all(held.at[:len(peers)], t_send.at[n], peers[0])
 
 
 def whole_kernel(
@@ -685,32 +744,41 @@
     inputs, queries, vectors, base, exps, coefs,
     att, mean_out, grad_out,
     xin, mg, vec_v, base_v, acc, hold, pout, pin, kv, rows_v, dkv, probs, logs, expos, outs, sums,
-    got, grads, held, held_t, q_v, att_v, io_sem, smem_sem, exps_v, coefs_v,
+    got, grads, q_v, att_v, io_sem, exps_v, coefs_v,
     local_sem, keep_sem, x_send, x_recv, y_send, y_recv, g_send, g_recv, r_send, r_recv, p_send, p_recv,
-    s_send, s_recv, d_send, d_recv, l_send, l_recv, t_send, t_recv, z_send, z_recv,
+    s_send, s_recv, d_send, d_recv, l_send, l_recv, u_send, t_send, t_recv, *helds,
 ):
     n_task = dims[0] * dims[1] * dims[2]
     task = lax.axis_index("task")
     y = lax.axis_index("tensor")
-    task_peers = [{"task": turned(task, s, n_task), "tensor": y} for s in range(1, n_task)]
-    tensor_peers = [{"task": task, "tensor": turned(y, s, n_tensor)} for s in range(1, n_tensor)]
-
-    small = [fetch(exps, exps_v, smem_sem.at[0]), fetch(coefs, coefs_v, smem_sem.at[1])]
+    if len(helds) == 1:
+        me, count = task * n_tensor + y, n_task * n_tensor
+        others = [turned(me, s, count) for s in range(1, count)]
+        groups = [
+            (me, [{"task": k // n_tensor, "tensor": lax.rem(k, n_tensor)} for k in others]),
+        ]
+    else:
+        groups = [
+            (task, [{"task": turned(task, s, n_task), "tensor": y} for s in range(1, n_task)]),
+            (y, [{"task": task, "tensor": turned(y, s, n_tensor)} for s in range(1, n_tensor)]),
+        ]
+
+    small = [fetch(exps, exps_v, io_sem.at[2]), fetch(coefs, coefs_v, io_sem.at[3])]
     waiting = []
 
     def greet():
-        meet(task_peers + tensor_peers)
+        meet([peer for _, peers in groups for peer in peers])
         for copy in small:
             copy.wait()
 
     query_copy = fetch(queries, q_v, io_sem.at[0])
-    sent, r_copies, keeps, keys_ready, between, values_ready = project_stage(
+    keys_ready, between, values_ready, rows_ready, drain = project_stage(
         dims, n_tensor, pieces, bunch, inputs, vectors, base, exps_v, coefs_v, greet, kv, rows_v,
         xin, mg, vec_v, base_v, acc, hold, pout, pin,
         local_sem, keep_sem, x_send, x_recv, y_send, y_recv, g_send, g_recv, r_send, r_recv, p_send, p_recv,
     )
     query_copy.wait()
-    plan = spread_plan(dims, kv.shape[0], dkv, got, d_send, d_recv, l_send, l_recv)
+    plan = spread_plan(dims, kv.shape[0], dkv, got, d_send, d_recv, l_send, l_recv, u_send)
 
     def att_done():
         waiting.append(fetch(att_v, att, io_sem.at[1]))
@@ -719,20 +787,13 @@
         n_tensor, q_v, kv, att_v, dkv, probs, logs, expos, outs, sums, s_send, s_recv,
         keys_ready, between, values_ready, att_done, plan[0],
     )
-
-    def rows_ready():
-        for copy in keeps:
-            copy.wait()
-        for copy in r_copies:
-            copy.wait_recv()
-
-    more = reduce_stage(
-        dims, n_tensor, task_peers, tensor_peers, rows_ready, entropy, plan,
+    reduce_stage(
+        dims, n_tensor, groups, rows_ready, entropy, plan,
         dkv, exps_v, grad_out, mean_out,
-        got, rows_v, vec_v, grads, held, held_t,
-        t_send, t_recv, z_send, z_recv,
+        got, rows_v, vec_v, grads, helds, t_send, t_recv,
     )
-    for copy in sent + r_copies + exchanged + more:
+    drain()
+    for copy in exchanged:
         copy.wait_send()
     for copy in waiting:
         copy.wait()
@@ -749,9 +810,11 @@
     heads = cols // HEAD
     pieces = math.gcd(tokens // 16, 6)
     bunch = math.gcd(pieces, 2)
-    hbm = pl.BlockSpec(memory_space=pl.ANY)
+    hbm = pl.BlockSpec(memory_space=pltpu.HBM)
+    anywhere = pl.BlockSpec(memory_space=pl.ANY)
     vmem = pl.BlockSpec(memory_space=pltpu.VMEM)
     dma = pltpu.SemaphoreType.DMA
+    slots = [n_task * n_tensor] if n_task * n_tensor <= 64 else [n_task, n_tensor]
 
     def pair(count):
         return [dma((count,)), dma((count,))]
@@ -764,7 +827,7 @@
             jax.ShapeDtypeStruct((mats, tasks), F32),
         ),
         in_specs=[hbm] * 6,
-        out_specs=(hbm, vmem, vmem),
+        out_specs=(anywhere, vmem, vmem),
         scratch_shapes=[
             pltpu.VMEM((outer, tokens, group * rows), BF16),
             pltpu.VMEM((group, mats, rows, cols), BF16),
@@ -784,30 +847,35 @@
             pltpu.VMEM((n_tensor, 8, tokens), F32),
             pltpu.VMEM((mats, n_task, tokens, cols), BF16),
             pltpu.VMEM((mats, rows, cols), F32),
-            pltpu.VMEM((n_task, 8, 128), F32),
-            pltpu.VMEM((n_tensor, 8, 128), F32),
             pltpu.VMEM(queries.shape, BF16),
             pltpu.VMEM(queries.shape, BF16),
-            dma((2,)),
-            dma((2,)),
+            dma((4,)),
             pltpu.SMEM((mats, *scale_exps.shape[2:], tasks), jnp.int32), pltpu.SMEM((mats, tasks), F32),
-            dma((2 + mats,)), dma((pieces * outer,)),
-            *pair(outer * pieces),
-            *pair(pieces * outer * n_tensor),
-            *pair(mats * group),
-            *pair((pieces // bunch) * n_task),
-            *pair(outer * pieces * mats),
+            dma((2 + mats,)), dma((1,)),
+            dma((1,)), dma((outer * pieces,)),
+            dma((1,)), dma((pieces,)),
+            dma((1,)), dma((mats * group,)),
+            dma((1,)), dma((1,)),
+            dma((1,)), dma((mats * (pieces + 2),)),
             *pair(n_tensor),
-            *pair(mats * n_task),
-            dma((mats * (outer + 1),)), dma((mats * outer,)),
-            *pair(n_task),
-            *pair(n_tensor),
+            dma((mats,)), dma((mats * n_task,)),
+            dma((1,)), dma((mats * outer,)),
+            dma((1,)),
+            *pair(len(slots)),
+            *[pltpu.VMEM((count, 1, 128), F32) for count in slots],
         ],
         compiler_params=pltpu.CompilerParams(
             collective_id=0, has_side_effects=True, vmem_limit_bytes=VMEM_BYTES
         ),
         name="whole",
-    )(inputs, queries, task_vectors, base_weights, scale_exps.transpose(1, 2, 3, 0), coefs.T)
+    )(
+        *[
+            pltpu.with_memory_space_constraint(value, pltpu.HBM)
+            for value in (
+                inputs, queries, task_vectors, base_weights, scale_exps.transpose(1, 2, 3, 0), coefs.T
+            )
+        ]
+    )
     return (attended, mean_entropy[0, 0], coef_grad.T)
 
 

time: 131 us -> 117 us (0.89)
  Pallas kernels: 126 us -> 113 us
  local copies, waits for them, and re-layouts: 3.32 us -> 1.45 us
    pallas_call x1, Pallas kernels: 126 us -> 113 us  [local(): pl.pallas_call(functools.partial(whole_kernel, dims, n_tensor, pieces, bu...]
    unnamed x2, local copies, waits for them, and re-layouts: 3.32 us -> 1.45 us
where the time goes in v2:
time: 117 us
  Pallas kernels  113 us (97%)
  between operations  2.33 us (2%)
  local copies, waits for them, and re-layouts  1.45 us (1%)
    pallas_call x1, Pallas kernels, local(): pl.pallas_call(functools.partial(whole_kernel, dims, n_tensor, pieces, bu...  113 us

profile of v2, /device:TPU:0, one launch (start us, length us, event | category | flops | bytes accessed | tf_op | source)
XLA Modules:
  0.0 117.2 jit_solution(10163549036060061116)
XLA Ops:
  0.6 113.4 %whole.1 = (bf16[192,2048]{1,0:T(8,128)(2,1)S(1)}, f32[1,1]{1,0:T(1,128)}, f32[2,8]{1,0:T(2,128)S(1)}) custom-call(bf16[192,8192]{1,0:T(8,128)(2,1)} %inputs.1, bf16[192,2048]{1,0:T(8,128)(2,1)} %queries.1, bf16[8,2,512,512]{3,2,1,0:T(8,128)(2,1)} %vectors.1, bf16[2,512,512]{2,1,0:T(8,128)(2,1)} %base.1, s32[2,4,4,8]{3,2,1,0:T(4,128)} %bitcast.5, f32[2,8]{1,0:T(2,128)} %bitcast.6), custom_call_target="tpu_custom_call" | custom-call | tf_op jit(solution)/shard_map/whole/pallas_call | solution.py:822
  114.1 0.9 copy.12
  115.5 0.6 copy.14

commit v3 on v2

--- a/solution.py
+++ b/solution.py
@@ -352,23 +352,19 @@
             parts_to(1, 1)
         if k == 3:
             parts_to(1, 2)
-        if k == 4:
-            parts_to(0, 3)
-            parts_to(1, 3)
-            combine_to(0, 1)
-        if k == 5:
-            parts_to(0, 4)
-            parts_to(1, 4)
-            combine_to(0, 2)
+        if k >= 4:
+            parts_to(0, k - 1)
+            parts_to(1, k - 1)
+            combine_to(0, k - 3)
     shared_up_to(mats - 1)
     parts_to(0, pieces - 1)
-    combine_to(0, 3)
+    combine_to(0, pieces - 3)
     parts_to(1, pieces - 1)
-    combine_to(0, 4)
+    combine_to(0, pieces - 2)
     parts_to(0, pieces)
     parts_to(1, pieces)
-    combine_to(0, 5)
-    combine_to(1, 2)
+    combine_to(0, pieces - 1)
+    combine_to(1, pieces - 4)
     combine_to(0, pieces)
 
     def keys_ready():
@@ -568,34 +564,54 @@
             device_id_type=MESH,
         )
         copies[m, slot] = copy
-        if not around:
-            copy.start()
-        elif k == 1:
-            guard(copy, 1 - inside)
+
+        def go():
+            if not around:
+                copy.start()
+            elif k == 1:
+                guard(copy, 1 - inside)
+
+        return go
 
     def sent_own(m):
         if outer > 1:
             guard(along(m, a, above), chosen(up, a))
             guard(along(m, a, below), chosen(down, a))
         for f in range(1, mid):
-            forward(m, 0, (0, 0), (f, 0))
+            forward(m, 0, (0, 0), (f, 0))()
         for e in range(1, inner):
-            forward(m, 0, (0, 0), (0, e))
-
-    def arrive(m, k):
+            forward(m, 0, (0, 0), (0, e))()
+
+    def arrive(m, k, which=None):
         _, target, valid = steps[k - 1]
         copy = along(m, planes[k], chosen(target, a))
-        copy.wait_recv()
-        guard(copy, chosen(valid, a))
-        for f in range(1, mid):
-            forward(m, k, (0, 0), (f, 0))
-        for e in range(1, inner):
-            forward(m, k, (0, 0), (0, e))
+        further = chosen(valid, a)
+        hops = [forward(m, k, (0, 0), (f, 0)) for f in range(1, mid)]
+        hops += [forward(m, k, (0, 0), (0, e)) for e in range(1, inner)]
+
+        def go():
+            copy.wait_recv()
+            guard(copy, further)
+            for hop in hops:
+                hop()
+
+        if which is None:
+            go()
+        else:
+            pl.when(inside == which)(go)
+
+    def come(m, k):
+        if k == 1:
+            arrive(m, 1)
+        else:
+            arrive(m, k, 0)
+        if k + 1 < outer:
+            arrive(m, k + 1, 1)
 
     def across(m, k, f):
         copies[m, (k, f, 0)].wait_recv()
         for e in range(1, inner):
-            forward(m, k, (f, 0), (0, e))
+            forward(m, k, (f, 0), (0, e))()
         if not detour or m != last:
             return
         if k == 0:
@@ -629,7 +645,7 @@
             def _():
                 sent_all(got.at[:, :1], l_send.at[0], peer)
 
-    return sent_own, arrive, across, core, source, drain
+    return sent_own, come, across, core, source, drain
 
 
 def reduce_stage(
@@ -643,13 +659,13 @@
     y = lax.axis_index("tensor")
     tasks, mats, rows, cols = vec_v.shape
     row_blocks, col_blocks = exps.shape[1:3]
-    _, arrive, across, core, source, drain = plan
+    _, come, across, core, source, drain = plan
     fresh = set()
 
     def take(m, k, f, e):
         own = not (k or f or e)
         if k and not (f or e):
-            arrive(m, k)
+            come(m, k)
         elif f and not e:
             across(m, k, f)
         elif e:
@@ -687,19 +703,20 @@
     rows_ready()
     lines = {}
     turns = [(k, m) for k in range(outer) for m in reversed(range(mats))]
+    across_turns = turns[:-mats] + turns[-mats:][::-1]
     for step in range(len(turns) + 2):
         slots = []
         if step < len(turns):
             slots.append((turns[step], 0, 0))
         if 1 <= step <= len(turns):
-            slots += [(turns[step - 1], f, 0) for f in range(1, mid)]
+            slots += [(across_turns[step - 1], f, 0) for f in range(1, mid)]
             slots += [(turns[step - 1], 0, e) for e in range(1, inner)]
         if step >= 2:
-            slots += [(turns[step - 2], f, e) for f in range(1, mid) for e in range(1, inner)]
+            slots += [(across_turns[step - 2], f, e) for f in range(1, mid) for e in range(1, inner)]
         for (k, m), f, e in slots:
             take(m, k, f, e)
         if step - 2 >= len(turns) - mats:
-            m = turns[step - 2][1]
+            m = across_turns[step - 2][1]
             lines[m] = contracted(m)
     parts = [
         jnp.sum(lines[m][t], axis=0, keepdims=True) for t in range(tasks) for m in range(mats)

time: 117 us -> 113 us (0.966)
  Pallas kernels: 113 us -> 110 us
    pallas_call x1, Pallas kernels: 113 us -> 110 us  [local(): pl.pallas_call(functools.partial(whole_kernel, dims, n_tensor, pieces, bu...]
where the time goes in v3:
time: 113 us
  Pallas kernels  110 us (97%)
  between operations  2.33 us (2%)
  local copies, waits for them, and re-layouts  1.45 us (1%)
    pallas_call x1, Pallas kernels, local(): pl.pallas_call(functools.partial(whole_kernel, dims, n_tensor, pieces, bu...  110 us

profile of v3, /device:TPU:0, one launch (start us, length us, event | category | flops | bytes accessed | tf_op | source)
XLA Modules:
  0.0 113.3 jit_solution(5757276190052923056)
XLA Ops:
  0.6 109.5 %whole.1 = (bf16[192,2048]{1,0:T(8,128)(2,1)S(1)}, f32[1,1]{1,0:T(1,128)}, f32[2,8]{1,0:T(2,128)S(1)}) custom-call(bf16[192,8192]{1,0:T(8,128)(2,1)} %inputs.1, bf16[192,2048]{1,0:T(8,128)(2,1)} %queries.1, bf16[8,2,512,512]{3,2,1,0:T(8,128)(2,1)} %vectors.1, bf16[2,512,512]{2,1,0:T(8,128)(2,1)} %base.1, s32[2,4,4,8]{3,2,1,0:T(4,128)} %bitcast.5, f32[2,8]{1,0:T(2,128)} %bitcast.6), custom_call_target="tpu_custom_call" | custom-call | tf_op jit(solution)/shard_map/whole/pallas_call | solution.py:839
  110.2 0.9 copy.12
  111.6 0.6 copy.14

commit v4 on v3

--- a/solution.py
+++ b/solution.py
@@ -705,19 +705,22 @@
     turns = [(k, m) for k in range(outer) for m in reversed(range(mats))]
     across_turns = turns[:-mats] + turns[-mats:][::-1]
     for step in range(len(turns) + 2):
-        slots = []
-        if step < len(turns):
-            slots.append((turns[step], 0, 0))
+        over = step >= len(turns)
+        first, then = [], []
+        if not over:
+            first.append((turns[step], 0, 0))
         if 1 <= step <= len(turns):
-            slots += [(across_turns[step - 1], f, 0) for f in range(1, mid)]
-            slots += [(turns[step - 1], 0, e) for e in range(1, inner)]
+            (then if over else first).extend([(across_turns[step - 1], f, 0) for f in range(1, mid)])
+            first += [(turns[step - 1], 0, e) for e in range(1, inner)]
         if step >= 2:
-            slots += [(across_turns[step - 2], f, e) for f in range(1, mid) for e in range(1, inner)]
-        for (k, m), f, e in slots:
+            first += [(across_turns[step - 2], f, e) for f in range(1, mid) for e in range(1, inner)]
+        for (k, m), f, e in first:
             take(m, k, f, e)
         if step - 2 >= len(turns) - mats:
             m = across_turns[step - 2][1]
             lines[m] = contracted(m)
+        for (k, m), f, e in then:
+            take(m, k, f, e)
     parts = [
         jnp.sum(lines[m][t], axis=0, keepdims=True) for t in range(tasks) for m in range(mats)
     ]

time: 113 us -> 114 us (level)
  no operation moved by 1% of the time
where the time goes in v4:
time: 114 us
  Pallas kernels  110 us (96%)
  between operations  2.33 us (2%)
  local copies, waits for them, and re-layouts  1.45 us (1%)
    pallas_call x1, Pallas kernels, local(): pl.pallas_call(functools.partial(whole_kernel, dims, n_tensor, pieces, bu...  110 us

profile of v4, /device:TPU:0, one launch (start us, length us, event | category | flops | bytes accessed | tf_op | source)
XLA Modules:
  0.0 113.9 jit_solution(9191702330750909664)
XLA Ops:
  0.6 110.1 %whole.1 = (bf16[192,2048]{1,0:T(8,128)(2,1)S(1)}, f32[1,1]{1,0:T(1,128)}, f32[2,8]{1,0:T(2,128)S(1)}) custom-call(bf16[192,8192]{1,0:T(8,128)(2,1)} %inputs.1, bf16[192,2048]{1,0:T(8,128)(2,1)} %queries.1, bf16[8,2,512,512]{3,2,1,0:T(8,128)(2,1)} %vectors.1, bf16[2,512,512]{2,1,0:T(8,128)(2,1)} %base.1, s32[2,4,4,8]{3,2,1,0:T(4,128)} %bitcast.5, f32[2,8]{1,0:T(2,128)} %bitcast.6), custom_call_target="tpu_custom_call" | custom-call | tf_op jit(solution)/shard_map/whole/pallas_call | solution.py:842
  110.7 0.9 copy.12
  112.2 0.6 copy.14
